TPU v7x, 32 devices: a whole 2x2x4 slice. The times are simulated.
32 devices in a mesh: step: 8 (over y, x, core), lat: 4 (over z).
Axes of the slice: x: 2, y: 2, z: 4, core: 2. Of those that a mesh axis runs over, the one named last changes fastest.
Arguments:
- state_in: bfloat16 [8, 72, 64, 128], P('step', None, 'lat'), may hold values from -6 to 6
- new_state: bfloat16 [72, 64, 128], P(None, 'lat'), may hold values from -6 to 6
- cot_early: bfloat16 [8, 72, 64, 128], P('step', None, 'lat'), may hold values from -6 to 6
- cot_late: bfloat16 [8, 72, 64, 128], P('step', None, 'lat'), may hold values from -6 to 6
- kernel_first: bfloat16 [9, 72, 192], replicated, may hold values from -0.25 to 0.25
- kernel_mid: bfloat16 [9, 192, 192], replicated, may hold values from -0.15625 to 0.15625
- kernel_last: bfloat16 [9, 72, 192], replicated, may hold values from -0.15625 to 0.15625
Outputs:
- advanced: bfloat16 [8, 72, 64, 128], P('step', None, 'lat')
- state_adjoint: bfloat16 [8, 72, 64, 128], P('step', None, 'lat')
- grad_first: float32 [9, 72, 192], replicated
- grad_mid: float32 [9, 192, 192], replicated
- grad_last: float32 [9, 72, 192], replicated
All inputs are finite; a program needn't handle non-finite values.
Results may differ from a plain program's by a relative error of at most 0.008.
Values may be sent and summed in bfloat16 or wider, within the bound.
A program may use at most 64 MiB of HBM per device.

v0:
```python
import math
import jax
import jax.numpy as jnp
from jax import lax
from jax.sharding import PartitionSpec as P


def padded_2(block, sides, width):
    for axis, dim in sides:
        count = lax.axis_size(axis)
        forward = [(i, i + 1) for i in range(count - 1)]
        backward = [(target, source) for source, target in forward]
        low = lax.ppermute(
            lax.slice_in_dim(block, block.shape[dim] - width, None, axis=dim), axis, forward
        )
        high = lax.ppermute(lax.slice_in_dim(block, 0, width, axis=dim), axis, backward)
        block = jnp.concatenate([low, block, high], axis=dim)
    return block


def shifted(block, axis, distance):
    devices = range(lax.axis_size(axis))
    route = [(i - distance, i) for i in devices if i - distance in devices]
    return lax.ppermute(block, axis, route)


def window_at(padded, dilation, row_tap, col_tap, out_rows, out_cols):
    widened = jnp.pad(padded, ((0, 0), (0, 0), (dilation, dilation)))
    return widened[
        :,
        row_tap * dilation : row_tap * dilation + out_rows,
        col_tap * dilation : col_tap * dilation + out_cols,
    ]


def convolve(padded, kernel, dilation, flipped):
    out_rows = padded.shape[1] - 2 * dilation
    out_cols = padded.shape[2]
    pattern = "oc,crw->orw" if flipped else "co,crw->orw"
    summed = None
    for tap_index in range(9):
        window = window_at(padded, dilation, tap_index // 3, tap_index % 3, out_rows, out_cols)
        product = jnp.einsum(pattern, kernel[tap_index], window, preferred_element_type=jnp.float32)
        summed = product if summed is None else summed + product
    return summed


def convolve_back(padded, kernel, dilation, flipped):
    out_rows = padded.shape[1] - 2 * dilation
    out_cols = padded.shape[2]
    pattern = "oc,orw->crw" if flipped else "co,orw->crw"
    summed = None
    for tap_index in range(9):
        window = window_at(
            padded, dilation, 2 - tap_index // 3, 2 - tap_index % 3, out_rows, out_cols
        )
        product = jnp.einsum(pattern, kernel[tap_index], window, preferred_element_type=jnp.float32)
        summed = product if summed is None else summed + product
    return summed


def kernel_terms(padded_in, grad_out, dilation, flipped):
    out_rows = grad_out.shape[1]
    out_cols = grad_out.shape[2]
    pattern = "crw,orw->oc" if flipped else "crw,orw->co"
    listed = []
    for tap_index in range(9):
        window = window_at(padded_in, dilation, tap_index // 3, tap_index % 3, out_rows, out_cols)
        listed.append(jnp.einsum(pattern, window, grad_out, preferred_element_type=jnp.float32))
    return jnp.stack(listed)


def gelu_slope(preact, cotangent):
    return jax.vjp(jax.nn.gelu, preact)[1](cotangent)[0]


def body(state_in, new_state, cot_early, cot_late, kernel_first, kernel_mid, kernel_last):
    band_rows = state_in.shape[2]
    total_rows = band_rows * lax.axis_size("lat")
    band_index = lax.axis_index("lat")

    def inside(values, margin):
        local_rows = jnp.arange(values.shape[1], dtype=jnp.int32)
        global_row = band_index * band_rows + local_rows - margin
        keep = (global_row >= 0) & (global_row < total_rows)
        return jnp.where(keep[None, :, None], values, jnp.zeros_like(values))

    def advance(state):
        extended = padded_2(state, (("lat", 1),), 7)
        pre_first = convolve(extended, kernel_first, 1, False)
        hid_first = inside(jax.nn.gelu(pre_first).astype(jnp.bfloat16), 6)
        pre_mid = convolve(hid_first, kernel_mid, 2, False)
        hid_mid = inside(jax.nn.gelu(pre_mid).astype(jnp.bfloat16), 4)
        pre_last = convolve(hid_mid, kernel_last, 4, True)
        saved = (
            extended[:, 6 : 6 + band_rows + 2],
            hid_first[:, 4 : 4 + band_rows + 4],
            hid_mid,
            pre_first[:, 6 : 6 + band_rows],
            pre_mid[:, 4 : 4 + band_rows],
        )
        output = (state.astype(jnp.float32) + pre_last).astype(jnp.bfloat16)
        return (output, saved)

    def backward(cot_out, saved):
        in_first, in_mid, in_last, pre_first, pre_mid = saved
        pad_last = padded_2(cot_out, (("lat", 1),), 4)
        back_mid = convolve_back(pad_last, kernel_last, 4, True)
        grads_last = kernel_terms(in_last, cot_out, 4, True)
        delta_mid = gelu_slope(pre_mid, back_mid).astype(jnp.bfloat16)
        pad_mid = padded_2(delta_mid, (("lat", 1),), 2)
        back_first = convolve_back(pad_mid, kernel_mid, 2, False)
        grads_mid = kernel_terms(in_mid, delta_mid, 2, False)
        delta_first = gelu_slope(pre_first, back_first).astype(jnp.bfloat16)
        pad_first = padded_2(delta_first, (("lat", 1),), 1)
        back_state = convolve_back(pad_first, kernel_first, 1, False)
        grads_first = kernel_terms(in_first, delta_first, 1, False)
        adjoint = (cot_out.astype(jnp.float32) + back_state).astype(jnp.bfloat16)
        return (adjoint, (grads_first, grads_mid, grads_last))

    early_out, early_saved = advance(state_in[0])
    passed = shifted(early_out, "step", 1)
    late_in = jnp.where(lax.axis_index("step") == 0, new_state, passed)
    late_out, late_saved = advance(late_in)
    late_adjoint, late_grads = backward(cot_late[0], late_saved)
    returned = shifted(late_adjoint, "step", -1)
    early_cot = (cot_early[0].astype(jnp.float32) + returned.astype(jnp.float32)).astype(
        jnp.bfloat16
    )
    state_adjoint, early_grads = backward(early_cot, early_saved)
    grand_total = lax.psum(
        (
            late_grads[0] + early_grads[0],
            late_grads[1] + early_grads[1],
            late_grads[2] + early_grads[2],
        ),
        ("step", "lat"),
    )
    cell_count = 2.0 * lax.axis_size("step") * total_rows * state_in.shape[3]
    grad_scale = 1.0 / math.sqrt(cell_count)
    return (
        late_out[None],
        state_adjoint[None],
        grand_total[0] * grad_scale,
        grand_total[1] * grad_scale,
        grand_total[2] * grad_scale,
    )


def solution(mesh):
    in_specs = (
        P("step", None, "lat", None),
        P(None, "lat", None),
        P("step", None, "lat", None),
        P("step", None, "lat", None),
        P(),
        P(),
        P(),
    )
    out_specs = (P("step", None, "lat", None), P("step", None, "lat", None), P(), P(), P())
    return jax.shard_map(body, mesh=mesh, in_specs=in_specs, out_specs=out_specs, check_vma=False)
```

profile of v0, /device:TPU:0, one launch (start us, length us, event | category | flops | bytes accessed | tf_op | source)
XLA Modules:
  0.0 348.6 jit_solution(4227039910495838793)
XLA Ops:
  7.2 1.1 copy.110
  8.4 5.0 %collective-permute-start = (bf16[72,7,128]{2,0,1:T(8,128)(2,1)S(1)}, bf16[72,7,128]{2,0,1:T(8,128)(2,1)S(1)}, u32[]{:S(2)}, u32[]{:S(2)}) collective-permute-start(bf16[72,7,128]{2,0,1:T(8,128)(2,1)S(1)} %get-tuple-element.27), channel_id=1, source_target_pairs={{0,1},{1,2},{2,3},{4,5},{5,6},{6,7},{8,9},{9,10},{10,11},{12,13},{... | collective-permute-start | bytes 387080 | tf_op jit(solution)/shard_map/ppermute | solution.py:13
  13.3 1.3 collective-permute-start.1
  14.6 1.0 copy.109
  15.7 4.5 %collective-permute-start.5 = (bf16[72,4,128]{2,0,1:T(8,128)(2,1)S(1)}, bf16[72,4,128]{2,0,1:T(8,128)(2,1)S(1)}, u32[]{:S(2)}, u32[]{:S(2)}) collective-permute-start(bf16[72,4,128]{2,0,1:T(8,128)(2,1)S(1)} %get-tuple-element.24), channel_id=1, source_target_pairs={{0,1},{1,2},{2,3},{4,5},{5,6},{6,7},{8,9},{9,10},{10,11},{12,13},{... | collective-permute-start | bytes 221192 | tf_op jit(solution)/shard_map/ppermute | solution.py:13
  20.3 1.3 collective-permute-start.6
  21.6 1.6 fusion.442
  23.2 3.3 collective-permute-done.6
  26.9 1.7 fusion.338
  28.6 1.6 fusion.340
  30.2 1.6 fusion.342
  31.8 1.6 fusion.344
  38.3 3.8 %fusion.75 = (bf16[192,28,128]{2,0,1:T(8,128)(2,1)S(1)}, f32[192,28,128]{2,0,1:T(8,128)}) fusion(pred[28]{0:T(512)(128)(4,1)S(1)} %compare_and_fusion, bf16[9,72,192]{2,1,0:T(8,128)(2,1)S(1)} %copy-done.8, bf16[72,30,128]{2,0,1:T(8,128)(2,1)S(1)} %pad_maximum_fusion, f32[28,128,192]{1,2,0:T(8,128)S(1)} %fusion.470, f32[28,128,192]{1,2,0:T(8,128)S(1)} %fusion.273, ...), kind=kOutput, calls=%fused_computation.167 | convolution fusion | flops 111476736 | bytes 26739200 | tf_op jit(solution)/shard_map/co,crw->orw/dot_general | solution.py:43
  46.5 3.3 fusion.129
  54.0 1.4 collective-permute-start.2
  55.4 1.5 fusion.305
  57.0 1.6 fusion.346
  58.7 3.5 collective-permute-start.3
  62.2 1.3 collective-permute-start.4
  63.5 1.5 fusion.309
  65.1 1.0 slice.996
  66.1 2.9 collective-permute-done.4
  73.4 1.3 fusion.468
  74.7 12.8 %fusion.74 = (bf16[192,28,128]{2,0,1:T(8,128)(2,1)S(1)}, f32[192,28,128]{2,0,1:T(8,128)}) fusion(pred[28]{0:T(512)(128)(4,1)S(1)} %compare_and_fusion, bf16[9,72,192]{2,1,0:T(8,128)(2,1)} %param.11, bf16[72,30,128]{2,0,1:T(8,128)(2,1)S(1)} %pad_maximum_fusion.1, f32[28,128,192]{1,2,0:T(8,128)S(1)} %fusion.468, f32[28,128,192]{1,2,0:T(8,128)S(1)} %fusion.279, ...), kind=kOutput, calls=%fused_computation.166 | convolution fusion | flops 111476736 | bytes 26738716 | tf_op jit(solution)/shard_map/co,crw->orw/dot_general | solution.py:43
  92.0 2.0 fusion.128
  94.0 6.1 %fusion.43 = bf16[192,16,128]{2,0,1:T(8,128)(2,1)S(1)} fusion(f32[16,128,192]{1,2,0:T(8,128)} %fusion.309, f32[16,128,192]{1,2,0:T(8,128)} %fusion.338, f32[16,128,192]{1,2,0:T(8,128)} %fusion.340, f32[192,16,128]{2,0,1:T(8,128)S(1)} %copy-done.6, f32[192,24,128]{2,0,1:T(8,128)S(1)} %get-tuple-element.36, f32[16,128,192]{1,2,0:T(8,128)} %fusion.342, ...), kind=kOutput, calls=%fused_computation.121 | convolution fusion | flops 67633152 | bytes 15273984 | tf_op jit(solution)/shard_map/oc,orw->crw/dot_general | solution.py:57
  103.6 1.3 collective-permute-start.8
  104.9 4.8 %collective-permute-start.7 = (bf16[192,2,128]{2,0,1:T(8,128)(2,1)S(1)}, bf16[192,2,128]{2,0,1:T(8,128)(2,1)S(1)}, u32[]{:S(2)}, u32[]{:S(2)}) collective-permute-start(bf16[192,2,128]{2,0,1:T(8,128)(2,1)S(1)} %get-tuple-element.20), channel_id=1, source_target_pairs={{0,1},{1,2},{2,3},{4,5},{5,6},{6,7},{8,9},{9,10},{10,11},{12,13},{... | collective-permute-start | bytes 294920 | tf_op jit(solution)/shard_map/ppermute | solution.py:13
  118.7 1.0 select_maximum_fusion.2
  122.7 1.0 copy-done.4
  123.8 1.7 fusion.50
  125.8 1.3 collective-permute-start.10
  127.1 5.0 %collective-permute-start.9 = (bf16[192,1,128]{2,0,1:T(8,128)(2,1)S(1)}, bf16[192,1,128]{2,0,1:T(8,128)(2,1)S(1)}, u32[]{:S(2)}, u32[]{:S(2)}) collective-permute-start(bf16[192,1,128]{2,0,1:T(8,128)(2,1)S(1)} %get-tuple-element.17), channel_id=1, source_target_pairs={{0,1},{1,2},{2,3},{4,5},{5,6},{6,7},{8,9},{9,10},{10,11},{12,13},{... | collective-permute-start | bytes 147464 | tf_op jit(solution)/shard_map/ppermute | solution.py:13
  138.7 1.4 collective-permute-start.11
  140.9 1.4 collective-permute-done.11
  146.1 1.3 collective-permute-start.13
  147.4 4.7 %collective-permute-start.12 = (bf16[72,4,128]{2,0,1:T(8,128)(2,1)S(1)}, bf16[72,4,128]{2,0,1:T(8,128)(2,1)S(1)}, u32[]{:S(2)}, u32[]{:S(2)}) collective-permute-start(bf16[72,4,128]{2,0,1:T(8,128)(2,1)S(1)} %get-tuple-element.22), channel_id=1, source_target_pairs={{0,1},{1,2},{2,3},{4,5},{5,6},{6,7},{8,9},{9,10},{10,11},{12,13},{... | collective-permute-start | bytes 221192 | tf_op jit(solution)/shard_map/ppermute | solution.py:13
  158.3 1.7 fusion.57
  164.6 1.3 collective-permute-start.15
  165.9 5.1 %collective-permute-start.14 = (bf16[192,2,128]{2,0,1:T(8,128)(2,1)S(1)}, bf16[192,2,128]{2,0,1:T(8,128)(2,1)S(1)}, u32[]{:S(2)}, u32[]{:S(2)}) collective-permute-start(bf16[192,2,128]{2,0,1:T(8,128)(2,1)S(1)} %get-tuple-element.16), channel_id=1, source_target_pairs={{0,1},{1,2},{2,3},{4,5},{5,6},{6,7},{8,9},{9,10},{10,11},{12,13},{... | collective-permute-start | bytes 294920 | tf_op jit(solution)/shard_map/ppermute | solution.py:13
  171.5 1.5 add.641
  173.0 1.0 select_maximum_fusion
  177.5 1.7 fusion.64
  182.5 1.3 collective-permute-start.17
  183.8 5.2 %collective-permute-start.16 = (bf16[192,1,128]{2,0,1:T(8,128)(2,1)S(1)}, bf16[192,1,128]{2,0,1:T(8,128)(2,1)S(1)}, u32[]{:S(2)}, u32[]{:S(2)}) collective-permute-start(bf16[192,1,128]{2,0,1:T(8,128)(2,1)S(1)} %get-tuple-element.13), channel_id=1, source_target_pairs={{0,1},{1,2},{2,3},{4,5},{5,6},{6,7},{8,9},{9,10},{10,11},{12,13},{... | collective-permute-start | bytes 147464 | tf_op jit(solution)/shard_map/ppermute | solution.py:13
  195.3 142.1 %all-reduce.19.cloned.1.call-done = (f32[9,72,192]{2,1,0:T(8,128)}, f32[9,192,192]{2,1,0:T(8,128)}, f32[9,72,192]{2,1,0:T(8,128)}) async-done(((f32[9,72,192]{2,1,0:T(8,128)}, f32[9,192,192]{2,1,0:T(8,128)}, f32[9,72,192]{2,1,0:T(8,128)}), (f32[9,72,192]{2,1,0:T(8,128)}, f32[9,192,192]{2,1,0:T(8,128)}, f32[9,72,192]{2,1,0:T(8,128)})) %all-reduce.19.cloned.1.call-update) | async-done | bytes 2322448 | tf_op jit(solution)/shard_map/psum | solution.py:131
  337.4 2.9 broadcast_multiply_fusion
  340.3 1.2 broadcast_multiply_fusion.1
  (246 shorter events, 73.4 us)
Async XLA Ops:
  7.2 14.4 %copy-start = (bf16[1,72,16,128]{3,2,1,0:T(8,128)(2,1)S(1)}, bf16[1,72,16,128]{3,2,1,0:T(8,128)(2,1)}, u32[]{:S(2)}) copy-start(bf16[1,72,16,128]{3,2,1,0:T(8,128)(2,1)} %param.10) | copy-start | bytes 884740
  7.2 14.4 %copy-start.7 = (bf16[9,72,192]{2,1,0:T(8,128)(2,1)S(1)}, bf16[9,72,192]{2,1,0:T(8,128)(2,1)}, u32[]{:S(2)}) copy-start(bf16[9,72,192]{2,1,0:T(8,128)(2,1)} %param.13) | copy-start | bytes 746500
  7.2 330.2 %all-reduce.19.cloned.1.call-start = ((), (), s32[]{:S(2)}) async-start(), calls=%async_computation | async-start | bytes 6193152 | tf_op jit(solution)/shard_map/psum | solution.py:131
  8.4 25.0 %collective-permute-start = (bf16[72,7,128]{2,0,1:T(8,128)(2,1)S(1)}, bf16[72,7,128]{2,0,1:T(8,128)(2,1)S(1)}, u32[]{:S(2)}, u32[]{:S(2)}) collective-permute-start(bf16[72,7,128]{2,0,1:T(8,128)(2,1)S(1)} %get-tuple-element.27), channel_id=1, source_target_pairs={{0,1},{1,2},{2,3},{4,5},{5,6},{6,7},{8,9},{9,10},{10,11},{12,13},{... | collective-permute-start | bytes 387080 | tf_op jit(solution)/shard_map/ppermute | solution.py:13
  13.3 20.0 %collective-permute-start.1 = (bf16[72,7,128]{2,0,1:T(8,128)(2,1)S(1)}, bf16[72,7,128]{2,0,1:T(8,128)(2,1)S(1)}, u32[]{:S(2)}, u32[]{:S(2)}) collective-permute-start(bf16[72,7,128]{2,0,1:T(8,128)(2,1)S(1)} %get-tuple-element.28), channel_id=1, source_target_pairs={{1,0},{2,1},{3,2},{5,4},{6,5},{7,6},{9,8},{10,9},{11,10},{13,12},{... | collective-permute-start | bytes 387080 | tf_op jit(solution)/shard_map/ppermute | solution.py:16
  15.7 7.5 %collective-permute-start.5 = (bf16[72,4,128]{2,0,1:T(8,128)(2,1)S(1)}, bf16[72,4,128]{2,0,1:T(8,128)(2,1)S(1)}, u32[]{:S(2)}, u32[]{:S(2)}) collective-permute-start(bf16[72,4,128]{2,0,1:T(8,128)(2,1)S(1)} %get-tuple-element.24), channel_id=1, source_target_pairs={{0,1},{1,2},{2,3},{4,5},{5,6},{6,7},{8,9},{9,10},{10,11},{12,13},{... | collective-permute-start | bytes 221192 | tf_op jit(solution)/shard_map/ppermute | solution.py:13
  20.3 6.2 %collective-permute-start.6 = (bf16[72,4,128]{2,0,1:T(8,128)(2,1)S(1)}, bf16[72,4,128]{2,0,1:T(8,128)(2,1)S(1)}, u32[]{:S(2)}, u32[]{:S(2)}) collective-permute-start(bf16[72,4,128]{2,0,1:T(8,128)(2,1)S(1)} %get-tuple-element.23), channel_id=1, source_target_pairs={{1,0},{2,1},{3,2},{5,4},{6,5},{7,6},{9,8},{10,9},{11,10},{13,12},{... | collective-permute-start | bytes 221192 | tf_op jit(solution)/shard_map/ppermute | solution.py:16
  23.2 5.4 %copy-start.26 = (bf16[72,4,128]{2,0,1:T(8,128)(2,1)}, bf16[72,4,128]{2,0,1:T(8,128)(2,1)S(1)}, u32[]{:S(2)}) copy-start(bf16[72,4,128]{2,0,1:T(8,128)(2,1)S(1)} %collective-permute-done.5) | copy-start | bytes 221188
  26.5 2.1 copy-start.28
  26.9 30.1 %copy-start.2 = (bf16[72,24,136]{2,0,1:T(8,128)(2,1)}, bf16[72,24,136]{2,0,1:T(8,128)(2,1)S(1)}, u32[]{:S(2)}) copy-start(bf16[72,24,136]{2,0,1:T(8,128)(2,1)S(1)} %select_maximum_fusion.10) | copy-start | bytes 1410052
  31.8 1.7 copy-start.8
  33.4 4.4 %copy-start.15 = (bf16[72,7,128]{2,0,1:T(8,128)(2,1)}, bf16[72,7,128]{2,0,1:T(8,128)(2,1)S(1)}, u32[]{:S(2)}) copy-start(bf16[72,7,128]{2,0,1:T(8,128)(2,1)S(1)} %collective-permute-done) | copy-start | bytes 387076
  33.4 4.4 %copy-start.13 = (bf16[72,7,128]{2,0,1:T(8,128)(2,1)}, bf16[72,7,128]{2,0,1:T(8,128)(2,1)S(1)}, u32[]{:S(2)}) copy-start(bf16[72,7,128]{2,0,1:T(8,128)(2,1)S(1)} %collective-permute-done.1) | copy-start | bytes 387076
  38.3 3.8 %copy-start.1 = (bf16[9,192,192]{2,1,0:T(8,128)(2,1)S(1)}, bf16[9,192,192]{2,1,0:T(8,128)(2,1)}, u32[]{:S(2)}) copy-start(bf16[9,192,192]{2,1,0:T(8,128)(2,1)} %param.12) | copy-start | bytes 1990660
  52.7 1.0 copy-start.11
  53.7 1.7 copy-start.29
  54.0 4.7 %copy-start.24 = (bf16[72,16,128]{2,1,0:T(8,128)(2,1)S(1)}, bf16[72,16,128]{2,1,0:T(8,128)(2,1)}, u32[]{:S(2)}) copy-start(bf16[72,16,128]{2,1,0:T(8,128)(2,1)} %param.8) | copy-start | bytes 884740
  54.0 4.6 %collective-permute-start.2 = (bf16[72,16,128]{2,0,1:T(8,128)(2,1)S(1)}, bf16[72,16,128]{2,0,1:T(8,128)(2,1)S(1)}, u32[]{:S(2)}, u32[]{:S(2)}) collective-permute-start(bf16[72,16,128]{2,0,1:T(8,128)(2,1)S(1)} %fusion.105), channel_id=1, source_target_pairs={{0,4},{4,8},{8,12},{12,16},{16,20},{20,24},{24,28},{1,5},{5,9},{9,... | collective-permute-start | bytes 884744 | tf_op jit(solution)/shard_map/ppermute | solution.py:24
  57.0 6.5 %copy-start.27 = (bf16[72,4,128]{2,0,1:T(8,128)(2,1)S(1)}, bf16[72,4,128]{2,0,1:T(8,128)(2,1)}, u32[]{:S(2)}) copy-start(bf16[72,4,128]{2,0,1:T(8,128)(2,1)} %copy-done.26) | copy-start | bytes 221188
  58.7 7.4 %collective-permute-start.3 = (bf16[72,7,128]{2,0,1:T(8,128)(2,1)S(1)}, bf16[72,7,128]{2,0,1:T(8,128)(2,1)S(1)}, u32[]{:S(2)}, u32[]{:S(2)}) collective-permute-start(bf16[72,7,128]{2,0,1:T(8,128)(2,1)S(1)} %get-tuple-element.25), channel_id=1, source_target_pairs={{0,1},{1,2},{2,3},{4,5},{5,6},{6,7},{8,9},{9,10},{10,11},{12,13},{... | collective-permute-start | bytes 387080 | tf_op jit(solution)/shard_map/ppermute | solution.py:13
  62.2 6.8 %collective-permute-start.4 = (bf16[72,7,128]{2,0,1:T(8,128)(2,1)S(1)}, bf16[72,7,128]{2,0,1:T(8,128)(2,1)S(1)}, u32[]{:S(2)}, u32[]{:S(2)}) collective-permute-start(bf16[72,7,128]{2,0,1:T(8,128)(2,1)S(1)} %get-tuple-element.26), channel_id=1, source_target_pairs={{1,0},{2,1},{3,2},{5,4},{6,5},{7,6},{9,8},{10,9},{11,10},{13,12},{... | collective-permute-start | bytes 387080 | tf_op jit(solution)/shard_map/ppermute | solution.py:16
  66.1 7.3 %copy-start.19 = (bf16[72,7,128]{2,0,1:T(8,128)(2,1)}, bf16[72,7,128]{2,0,1:T(8,128)(2,1)S(1)}, u32[]{:S(2)}) copy-start(bf16[72,7,128]{2,0,1:T(8,128)(2,1)S(1)} %collective-permute-done.3) | copy-start | bytes 387076
  69.1 4.3 %copy-start.17 = (bf16[72,7,128]{2,0,1:T(8,128)(2,1)}, bf16[72,7,128]{2,0,1:T(8,128)(2,1)S(1)}, u32[]{:S(2)}) copy-start(bf16[72,7,128]{2,0,1:T(8,128)(2,1)S(1)} %collective-permute-done.4) | copy-start | bytes 387076
  92.0 2.0 copy-start.6
  103.6 15.1 %collective-permute-start.8 = (bf16[192,2,128]{2,0,1:T(8,128)(2,1)S(1)}, bf16[192,2,128]{2,0,1:T(8,128)(2,1)S(1)}, u32[]{:S(2)}, u32[]{:S(2)}) collective-permute-start(bf16[192,2,128]{2,0,1:T(8,128)(2,1)S(1)} %get-tuple-element.19), channel_id=1, source_target_pairs={{1,0},{2,1},{3,2},{5,4},{6,5},{7,6},{9,8},{10,9},{11,10},{13,12},{... | collective-permute-start | bytes 294920 | tf_op jit(solution)/shard_map/ppermute | solution.py:16
  104.9 13.8 %collective-permute-start.7 = (bf16[192,2,128]{2,0,1:T(8,128)(2,1)S(1)}, bf16[192,2,128]{2,0,1:T(8,128)(2,1)S(1)}, u32[]{:S(2)}, u32[]{:S(2)}) collective-permute-start(bf16[192,2,128]{2,0,1:T(8,128)(2,1)S(1)} %get-tuple-element.20), channel_id=1, source_target_pairs={{0,1},{1,2},{2,3},{4,5},{5,6},{6,7},{8,9},{9,10},{10,11},{12,13},{... | collective-permute-start | bytes 294920 | tf_op jit(solution)/shard_map/ppermute | solution.py:13
  122.0 1.8 copy-start.4
  123.8 1.7 copy-start.9
  125.5 7.0 %copy-start.20 = (bf16[72,7,128]{2,0,1:T(8,128)(2,1)S(1)}, bf16[72,7,128]{2,0,1:T(8,128)(2,1)}, u32[]{:S(2)}) copy-start(bf16[72,7,128]{2,0,1:T(8,128)(2,1)} %copy-done.19) | copy-start | bytes 387076
  125.8 9.1 %collective-permute-start.10 = (bf16[192,1,128]{2,0,1:T(8,128)(2,1)S(1)}, bf16[192,1,128]{2,0,1:T(8,128)(2,1)S(1)}, u32[]{:S(2)}, u32[]{:S(2)}) collective-permute-start(bf16[192,1,128]{2,0,1:T(8,128)(2,1)S(1)} %get-tuple-element.18), channel_id=1, source_target_pairs={{1,0},{2,1},{3,2},{5,4},{6,5},{7,6},{9,8},{10,9},{11,10},{13,12},{... | collective-permute-start | bytes 147464 | tf_op jit(solution)/shard_map/ppermute | solution.py:16
  127.1 7.8 %collective-permute-start.9 = (bf16[192,1,128]{2,0,1:T(8,128)(2,1)S(1)}, bf16[192,1,128]{2,0,1:T(8,128)(2,1)S(1)}, u32[]{:S(2)}, u32[]{:S(2)}) collective-permute-start(bf16[192,1,128]{2,0,1:T(8,128)(2,1)S(1)} %get-tuple-element.17), channel_id=1, source_target_pairs={{0,1},{1,2},{2,3},{4,5},{5,6},{6,7},{8,9},{9,10},{10,11},{12,13},{... | collective-permute-start | bytes 147464 | tf_op jit(solution)/shard_map/ppermute | solution.py:13
  138.3 1.8 copy-start.18
  138.6 3.6 %copy-start.25 = (bf16[1,72,16,128]{3,2,1,0:T(8,128)(2,1)S(1)}, bf16[1,72,16,128]{3,2,1,0:T(8,128)(2,1)}, u32[]{:S(2)}) copy-start(bf16[1,72,16,128]{3,2,1,0:T(8,128)(2,1)} %param.9) | copy-start | bytes 884740
  138.7 3.6 %collective-permute-start.11 = (bf16[72,16,128]{2,0,1:T(8,128)(2,1)S(1)}, bf16[72,16,128]{2,0,1:T(8,128)(2,1)S(1)}, u32[]{:S(2)}, u32[]{:S(2)}) collective-permute-start(bf16[72,16,128]{2,0,1:T(8,128)(2,1)S(1)} %fusion.104), channel_id=1, source_target_pairs={{4,0},{8,4},{12,8},{16,12},{20,16},{24,20},{28,24},{5,1},{9,5},{13... | collective-permute-start | bytes 884744 | tf_op jit(solution)/shard_map/ppermute | solution.py:24
  146.1 7.4 %collective-permute-start.13 = (bf16[72,4,128]{2,0,1:T(8,128)(2,1)S(1)}, bf16[72,4,128]{2,0,1:T(8,128)(2,1)S(1)}, u32[]{:S(2)}, u32[]{:S(2)}) collective-permute-start(bf16[72,4,128]{2,0,1:T(8,128)(2,1)S(1)} %get-tuple-element.21), channel_id=1, source_target_pairs={{1,0},{2,1},{3,2},{5,4},{6,5},{7,6},{9,8},{10,9},{11,10},{13,12},{... | collective-permute-start | bytes 221192 | tf_op jit(solution)/shard_map/ppermute | solution.py:16
  147.4 6.5 %collective-permute-start.12 = (bf16[72,4,128]{2,0,1:T(8,128)(2,1)S(1)}, bf16[72,4,128]{2,0,1:T(8,128)(2,1)S(1)}, u32[]{:S(2)}, u32[]{:S(2)}) collective-permute-start(bf16[72,4,128]{2,0,1:T(8,128)(2,1)S(1)} %get-tuple-element.22), channel_id=1, source_target_pairs={{0,1},{1,2},{2,3},{4,5},{5,6},{6,7},{8,9},{9,10},{10,11},{12,13},{... | collective-permute-start | bytes 221192 | tf_op jit(solution)/shard_map/ppermute | solution.py:13
  156.6 1.7 copy-start.5
  160.0 1.2 copy-start.21
  164.6 8.4 %collective-permute-start.15 = (bf16[192,2,128]{2,0,1:T(8,128)(2,1)S(1)}, bf16[192,2,128]{2,0,1:T(8,128)(2,1)S(1)}, u32[]{:S(2)}, u32[]{:S(2)}) collective-permute-start(bf16[192,2,128]{2,0,1:T(8,128)(2,1)S(1)} %get-tuple-element.15), channel_id=1, source_target_pairs={{1,0},{2,1},{3,2},{5,4},{6,5},{7,6},{9,8},{10,9},{11,10},{13,12},{... | collective-permute-start | bytes 294920 | tf_op jit(solution)/shard_map/ppermute | solution.py:16
  165.9 7.1 %collective-permute-start.14 = (bf16[192,2,128]{2,0,1:T(8,128)(2,1)S(1)}, bf16[192,2,128]{2,0,1:T(8,128)(2,1)S(1)}, u32[]{:S(2)}, u32[]{:S(2)}) collective-permute-start(bf16[192,2,128]{2,0,1:T(8,128)(2,1)S(1)} %get-tuple-element.16), channel_id=1, source_target_pairs={{0,1},{1,2},{2,3},{4,5},{5,6},{6,7},{8,9},{9,10},{10,11},{12,13},{... | collective-permute-start | bytes 294920 | tf_op jit(solution)/shard_map/ppermute | solution.py:13
  175.7 1.8 copy-start.3
  180.1 1.2 copy-start.12
  181.3 7.7 %copy-start.14 = (bf16[72,7,128]{2,0,1:T(8,128)(2,1)S(1)}, bf16[72,7,128]{2,0,1:T(8,128)(2,1)}, u32[]{:S(2)}) copy-start(bf16[72,7,128]{2,0,1:T(8,128)(2,1)} %copy-done.13) | copy-start | bytes 387076
  182.5 8.3 %collective-permute-start.17 = (bf16[192,1,128]{2,0,1:T(8,128)(2,1)S(1)}, bf16[192,1,128]{2,0,1:T(8,128)(2,1)S(1)}, u32[]{:S(2)}, u32[]{:S(2)}) collective-permute-start(bf16[192,1,128]{2,0,1:T(8,128)(2,1)S(1)} %get-tuple-element.14), channel_id=1, source_target_pairs={{1,0},{2,1},{3,2},{5,4},{6,5},{7,6},{9,8},{10,9},{11,10},{13,12},{... | collective-permute-start | bytes 147464 | tf_op jit(solution)/shard_map/ppermute | solution.py:16
  183.8 7.0 %collective-permute-start.16 = (bf16[192,1,128]{2,0,1:T(8,128)(2,1)S(1)}, bf16[192,1,128]{2,0,1:T(8,128)(2,1)S(1)}, u32[]{:S(2)}, u32[]{:S(2)}) collective-permute-start(bf16[192,1,128]{2,0,1:T(8,128)(2,1)S(1)} %get-tuple-element.13), channel_id=1, source_target_pairs={{0,1},{1,2},{2,3},{4,5},{5,6},{6,7},{8,9},{9,10},{10,11},{12,13},{... | collective-permute-start | bytes 147464 | tf_op jit(solution)/shard_map/ppermute | solution.py:13
  190.7 1.0 copy-start.10
  337.4 2.9 copy-start.22
  337.4 2.9 copy-start.23
  (1 other events, 0.9 us)
Sparse Core Ops, SparseCore 0:
  190.9 146.4 all-reduce.18
where the time goes:
time: 355 us; the launch traced here: 349 us
  waiting for transfers between devices  150 us (42%)
  matrix products  110 us (31%)
  starting transfers between devices  51 us (14%)
  between operations  15.7 us (4%)
  other arithmetic  12.5 us (4%)
  local copies, waits for them, and re-layouts  9.15 us (3%)
    psum x1, waiting for transfers between devices, body(): lax.psum((late_grads[0] + early_grads[0], late_grads[1] + early_grads[1],...  142 us
    dot_general x54, matrix products, convolve(): jnp.einsum(pattern, kernel[tap_index], window, preferred_element_type=jnp...  47.8 us
    dot_general x54, matrix products, convolve_back(): jnp.einsum(pattern, kernel[tap_index], window, preferred_element_type=jnp...  39.9 us
    ppermute x8, starting transfers between devices, padded_2(): lax.ppermute(lax.slice_in_dim(block, block.shape[dim] - width, None, axis...  37.7 us
    dot_general x54, matrix products, kernel_terms(): jnp.einsum(pattern, window, grad_out, preferred_element_type=jnp.float32)  22.5 us
    ppermute x8, starting transfers between devices, padded_2(): lax.ppermute(lax.slice_in_dim(block, 0, width, axis=dim), axis, backward)  10.3 us
    unnamed x64, local copies, waits for them, and re-layouts  7.89 us
  transfers between devices with their start and end apart: 19, of which 5 were waited for; matrix products, arithmetic and copies ran while one was open for 11% of the time, Pallas kernels for 0%

commit v1 on v0

--- a/solution.py
+++ b/solution.py
@@ -129,12 +129,15 @@
     )
     state_adjoint, early_grads = backward(early_cot, early_saved)
     grand_total = lax.psum(
-        (
-            late_grads[0] + early_grads[0],
-            late_grads[1] + early_grads[1],
-            late_grads[2] + early_grads[2],
+        lax.psum(
+            (
+                late_grads[0] + early_grads[0],
+                late_grads[1] + early_grads[1],
+                late_grads[2] + early_grads[2],
+            ),
+            "lat",
         ),
-        ("step", "lat"),
+        "step",
     )
     cell_count = 2.0 * lax.axis_size("step") * total_rows * state_in.shape[3]
     grad_scale = 1.0 / math.sqrt(cell_count)

time: 355 us -> 395 us (1.11)
  waiting for transfers between devices: 150 us -> 190 us
    psum x0 -> x1, waiting for transfers between devices: none -> 68.2 us  [body(): lax.psum(lax.psum((late_grads[0] + early_grads[0], late_grads[1] + early_...]
    psum x1, waiting for transfers between devices: 142 us -> 113 us  [body(): lax.psum((late_grads[0] + early_grads[0], late_grads[1] + early_grads[1],...]
    unnamed x64 -> x76, local copies, waits for them, and re-layouts: 7.89 us -> 8.41 us
  transfers between devices with their start and end apart: 19 -> 20, of which waited for: 5 -> 7; matrix products, arithmetic and copies ran while one was open for 11% -> 11% of each run, Pallas kernels for 0% -> 0%
where the time goes in v1:
time: 395 us; the launch traced here: 389 us
  waiting for transfers between devices  190 us (48%)
  matrix products  110 us (28%)
  starting transfers between devices  51 us (13%)
  between operations  15.8 us (4%)
  other arithmetic  12.5 us (3%)
  local copies, waits for them, and re-layouts  9.69 us (2%)
    psum x1, waiting for transfers between devices, body(): lax.psum((late_grads[0] + early_grads[0], late_grads[1] + early_grads[1],...  113 us
    psum x1, waiting for transfers between devices, body(): lax.psum(lax.psum((late_grads[0] + early_grads[0], late_grads[1] + early_...  68.2 us
    dot_general x54, matrix products, convolve(): jnp.einsum(pattern, kernel[tap_index], window, preferred_element_type=jnp...  45.3 us
    dot_general x54, matrix products, convolve_back(): jnp.einsum(pattern, kernel[tap_index], window, preferred_element_type=jnp...  41.8 us
    ppermute x8, starting transfers between devices, padded_2(): lax.ppermute(lax.slice_in_dim(block, block.shape[dim] - width, None, axis...  37.7 us
    dot_general x54, matrix products, kernel_terms(): jnp.einsum(pattern, window, grad_out, preferred_element_type=jnp.float32)  22.5 us
    ppermute x8, starting transfers between devices, padded_2(): lax.ppermute(lax.slice_in_dim(block, 0, width, axis=dim), axis, backward)  10.3 us
    unnamed x76, local copies, waits for them, and re-layouts  8.41 us
  transfers between devices with their start and end apart: 20, of which 7 were waited for; matrix products, arithmetic and copies ran while one was open for 11% of the time, Pallas kernels for 0%

profile of v1, /device:TPU:0, one launch (start us, length us, event | category | flops | bytes accessed | tf_op | source)
XLA Modules:
  0.0 388.5 jit_solution(7350537511024041613)
XLA Ops:
  8.4 5.0 %collective-permute-start = (bf16[72,7,128]{2,0,1:T(8,128)(2,1)S(1)}, bf16[72,7,128]{2,0,1:T(8,128)(2,1)S(1)}, u32[]{:S(2)}, u32[]{:S(2)}) collective-permute-start(bf16[72,7,128]{2,0,1:T(8,128)(2,1)S(1)} %get-tuple-element.30), channel_id=1, source_target_pairs={{0,1},{1,2},{2,3},{4,5},{5,6},{6,7},{8,9},{9,10},{10,11},{12,13},{... | collective-permute-start | bytes 387080 | tf_op jit(solution)/shard_map/ppermute | solution.py:13
  13.3 1.3 collective-permute-start.1
  15.7 4.5 %collective-permute-start.5 = (bf16[72,4,128]{2,0,1:T(8,128)(2,1)S(1)}, bf16[72,4,128]{2,0,1:T(8,128)(2,1)S(1)}, u32[]{:S(2)}, u32[]{:S(2)}) collective-permute-start(bf16[72,4,128]{2,0,1:T(8,128)(2,1)S(1)} %get-tuple-element.27), channel_id=1, source_target_pairs={{0,1},{1,2},{2,3},{4,5},{5,6},{6,7},{8,9},{9,10},{10,11},{12,13},{... | collective-permute-start | bytes 221192 | tf_op jit(solution)/shard_map/ppermute | solution.py:13
  20.3 1.3 collective-permute-start.6
  21.6 1.6 fusion.442
  23.2 3.3 collective-permute-done.6
  27.0 1.6 fusion.338
  28.6 1.6 fusion.340
  30.2 1.6 fusion.342
  31.8 1.6 fusion.344
  37.7 1.4 fusion.470
  39.2 4.0 %fusion.75 = (bf16[192,28,128]{2,0,1:T(8,128)(2,1)S(1)}, f32[192,28,128]{2,0,1:T(8,128)}) fusion(pred[28]{0:T(512)(128)(4,1)S(1)} %compare_and_fusion, bf16[9,72,192]{2,1,0:T(8,128)(2,1)S(1)} %copy-done.15, bf16[72,30,128]{2,0,1:T(8,128)(2,1)S(1)} %pad_maximum_fusion, f32[28,128,192]{1,2,0:T(8,128)S(1)} %fusion.470, f32[28,128,192]{1,2,0:T(8,128)S(1)} %fusion.273, ...), kind=kOutput, calls=%fused_computation.167 | convolution fusion | flops 111476736 | bytes 26739200 | tf_op jit(solution)/shard_map/co,crw->orw/dot_general | solution.py:43
  47.6 3.3 fusion.129
  55.1 1.4 collective-permute-start.2
  56.5 1.6 fusion.305
  58.1 1.6 fusion.346
  59.8 3.5 collective-permute-start.3
  63.3 1.3 collective-permute-start.4
  64.6 1.5 fusion.309
  67.3 2.9 collective-permute-done.4
  73.9 1.3 fusion.488
  75.3 1.3 fusion.468
  76.6 4.4 %fusion.74 = (bf16[192,28,128]{2,0,1:T(8,128)(2,1)S(1)}, f32[192,28,128]{2,0,1:T(8,128)}) fusion(pred[28]{0:T(512)(128)(4,1)S(1)} %compare_and_fusion, bf16[9,72,192]{2,1,0:T(8,128)(2,1)} %param.11, bf16[72,30,128]{2,0,1:T(8,128)(2,1)S(1)} %pad_maximum_fusion.1, f32[28,128,192]{1,2,0:T(8,128)S(1)} %fusion.468, f32[28,128,192]{1,2,0:T(8,128)S(1)} %fusion.279, ...), kind=kOutput, calls=%fused_computation.166 | convolution fusion | flops 111476736 | bytes 26738716 | tf_op jit(solution)/shard_map/co,crw->orw/dot_general | solution.py:43
  85.5 2.1 fusion.128
  87.5 6.0 %fusion.43 = bf16[192,16,128]{2,0,1:T(8,128)(2,1)S(1)} fusion(f32[16,128,192]{1,2,0:T(8,128)} %fusion.309, f32[16,128,192]{1,2,0:T(8,128)} %fusion.338, f32[16,128,192]{1,2,0:T(8,128)} %fusion.340, f32[192,16,128]{2,0,1:T(8,128)S(1)} %copy-done.10, f32[192,24,128]{2,0,1:T(8,128)S(1)} %get-tuple-element.39, f32[16,128,192]{1,2,0:T(8,128)} %fusion.342, ...), kind=kOutput, calls=%fused_computation.121 | convolution fusion | flops 67633152 | bytes 15273984 | tf_op jit(solution)/shard_map/oc,orw->crw/dot_general | solution.py:57
  96.2 1.3 collective-permute-start.8
  97.5 4.8 %collective-permute-start.7 = (bf16[192,2,128]{2,0,1:T(8,128)(2,1)S(1)}, bf16[192,2,128]{2,0,1:T(8,128)(2,1)S(1)}, u32[]{:S(2)}, u32[]{:S(2)}) collective-permute-start(bf16[192,2,128]{2,0,1:T(8,128)(2,1)S(1)} %get-tuple-element.23), channel_id=1, source_target_pairs={{0,1},{1,2},{2,3},{4,5},{5,6},{6,7},{8,9},{9,10},{10,11},{12,13},{... | collective-permute-start | bytes 294920 | tf_op jit(solution)/shard_map/ppermute | solution.py:13
  115.8 1.7 fusion.50
  117.8 1.3 collective-permute-start.10
  119.1 5.0 %collective-permute-start.9 = (bf16[192,1,128]{2,0,1:T(8,128)(2,1)S(1)}, bf16[192,1,128]{2,0,1:T(8,128)(2,1)S(1)}, u32[]{:S(2)}, u32[]{:S(2)}) collective-permute-start(bf16[192,1,128]{2,0,1:T(8,128)(2,1)S(1)} %get-tuple-element.20), channel_id=1, source_target_pairs={{0,1},{1,2},{2,3},{4,5},{5,6},{6,7},{8,9},{9,10},{10,11},{12,13},{... | collective-permute-start | bytes 147464 | tf_op jit(solution)/shard_map/ppermute | solution.py:13
  130.7 1.4 collective-permute-start.11
  132.9 1.4 collective-permute-done.11
  138.2 1.3 collective-permute-start.13
  139.5 4.7 %collective-permute-start.12 = (bf16[72,4,128]{2,0,1:T(8,128)(2,1)S(1)}, bf16[72,4,128]{2,0,1:T(8,128)(2,1)S(1)}, u32[]{:S(2)}, u32[]{:S(2)}) collective-permute-start(bf16[72,4,128]{2,0,1:T(8,128)(2,1)S(1)} %get-tuple-element.25), channel_id=1, source_target_pairs={{0,1},{1,2},{2,3},{4,5},{5,6},{6,7},{8,9},{9,10},{10,11},{12,13},{... | collective-permute-start | bytes 221192 | tf_op jit(solution)/shard_map/ppermute | solution.py:13
  150.4 1.7 fusion.57
  156.6 1.3 collective-permute-start.15
  157.9 5.1 %collective-permute-start.14 = (bf16[192,2,128]{2,0,1:T(8,128)(2,1)S(1)}, bf16[192,2,128]{2,0,1:T(8,128)(2,1)S(1)}, u32[]{:S(2)}, u32[]{:S(2)}) collective-permute-start(bf16[192,2,128]{2,0,1:T(8,128)(2,1)S(1)} %get-tuple-element.19), channel_id=1, source_target_pairs={{0,1},{1,2},{2,3},{4,5},{5,6},{6,7},{8,9},{9,10},{10,11},{12,13},{... | collective-permute-start | bytes 294920 | tf_op jit(solution)/shard_map/ppermute | solution.py:13
  163.5 1.5 add.647
  169.6 1.7 fusion.64
  175.9 1.3 fusion.303
  177.2 1.2 fusion.304
  181.2 1.3 collective-permute-start.17
  182.8 5.2 %collective-permute-start.16 = (bf16[192,1,128]{2,0,1:T(8,128)(2,1)S(1)}, bf16[192,1,128]{2,0,1:T(8,128)(2,1)S(1)}, u32[]{:S(2)}, u32[]{:S(2)}) collective-permute-start(bf16[192,1,128]{2,0,1:T(8,128)(2,1)S(1)} %get-tuple-element.16), channel_id=1, source_target_pairs={{0,1},{1,2},{2,3},{4,5},{5,6},{6,7},{8,9},{9,10},{10,11},{12,13},{... | collective-permute-start | bytes 147464 | tf_op jit(solution)/shard_map/ppermute | solution.py:13
  191.9 113.4 %all-reduce.23.cloned.1.call-done = (f32[9,72,192]{2,1,0:T(8,128)}, f32[9,192,192]{2,1,0:T(8,128)}, f32[9,72,192]{2,1,0:T(8,128)}) async-done(((f32[9,72,192]{2,1,0:T(8,128)}, f32[9,192,192]{2,1,0:T(8,128)}, f32[9,72,192]{2,1,0:T(8,128)}), (f32[9,72,192]{2,1,0:T(8,128)}, f32[9,192,192]{2,1,0:T(8,128)}, f32[9,72,192]{2,1,0:T(8,128)})) %all-reduce.23.cloned.1.call-update) | async-done | bytes 2322448 | tf_op jit(solution)/shard_map/psum | solution.py:132
  305.6 1.5 fusion.220
  309.2 68.2 %all-reduce.21.cloned.1.call-done = (f32[9,72,192]{2,1,0:T(8,128)}, f32[9,192,192]{2,1,0:T(8,128)}, f32[9,72,192]{2,1,0:T(8,128)}) async-done(((f32[9,72,192]{2,1,0:T(8,128)}, f32[9,192,192]{2,1,0:T(8,128)}, f32[9,72,192]{2,1,0:T(8,128)}), (f32[9,72,192]{2,1,0:T(8,128)}, f32[9,192,192]{2,1,0:T(8,128)}, f32[9,72,192]{2,1,0:T(8,128)})) %all-reduce.21.cloned.1.call-update) | async-done | bytes 2322448 | tf_op jit(solution)/shard_map/psum | solution.py:131
  377.3 2.9 broadcast_multiply_fusion
  380.3 1.2 broadcast_multiply_fusion.1
  (261 shorter events, 81.6 us)
Async XLA Ops:
  7.2 14.4 %copy-start = (bf16[1,72,16,128]{3,2,1,0:T(8,128)(2,1)S(1)}, bf16[1,72,16,128]{3,2,1,0:T(8,128)(2,1)}, u32[]{:S(2)}) copy-start(bf16[1,72,16,128]{3,2,1,0:T(8,128)(2,1)} %param.10) | copy-start | bytes 884740
  7.2 14.4 %copy-start.13 = (bf16[9,72,192]{2,1,0:T(8,128)(2,1)S(1)}, bf16[9,72,192]{2,1,0:T(8,128)(2,1)}, u32[]{:S(2)}) copy-start(bf16[9,72,192]{2,1,0:T(8,128)(2,1)} %param.13) | copy-start | bytes 746500
  7.2 298.1 %all-reduce.23.cloned.1.call-start = ((), (), s32[]{:S(2)}) async-start(), calls=%async_computation.1 | async-start | bytes 6193152 | tf_op jit(solution)/shard_map/psum | solution.py:132
  8.3 29.4 %copy-start.4 = (bf16[1,72,16,128]{3,1,2,0:T(8,128)(2,1)}, bf16[1,72,16,128]{3,1,2,0:T(8,128)(2,1)S(1)}, u32[]{:S(2)}) copy-start(bf16[1,72,16,128]{3,1,2,0:T(8,128)(2,1)S(1)} %copy.110) | copy-start | bytes 884740
  8.4 25.0 %collective-permute-start = (bf16[72,7,128]{2,0,1:T(8,128)(2,1)S(1)}, bf16[72,7,128]{2,0,1:T(8,128)(2,1)S(1)}, u32[]{:S(2)}, u32[]{:S(2)}) collective-permute-start(bf16[72,7,128]{2,0,1:T(8,128)(2,1)S(1)} %get-tuple-element.30), channel_id=1, source_target_pairs={{0,1},{1,2},{2,3},{4,5},{5,6},{6,7},{8,9},{9,10},{10,11},{12,13},{... | collective-permute-start | bytes 387080 | tf_op jit(solution)/shard_map/ppermute | solution.py:13
  13.3 20.0 %collective-permute-start.1 = (bf16[72,7,128]{2,0,1:T(8,128)(2,1)S(1)}, bf16[72,7,128]{2,0,1:T(8,128)(2,1)S(1)}, u32[]{:S(2)}, u32[]{:S(2)}) collective-permute-start(bf16[72,7,128]{2,0,1:T(8,128)(2,1)S(1)} %get-tuple-element.31), channel_id=1, source_target_pairs={{1,0},{2,1},{3,2},{5,4},{6,5},{7,6},{9,8},{10,9},{11,10},{13,12},{... | collective-permute-start | bytes 387080 | tf_op jit(solution)/shard_map/ppermute | solution.py:16
  15.7 11.3 %copy-start.11 = (bf16[1,72,16,128]{3,1,2,0:T(8,128)(2,1)}, bf16[1,72,16,128]{3,1,2,0:T(8,128)(2,1)S(1)}, u32[]{:S(2)}) copy-start(bf16[1,72,16,128]{3,1,2,0:T(8,128)(2,1)S(1)} %copy.109) | copy-start | bytes 884740
  15.7 7.5 %collective-permute-start.5 = (bf16[72,4,128]{2,0,1:T(8,128)(2,1)S(1)}, bf16[72,4,128]{2,0,1:T(8,128)(2,1)S(1)}, u32[]{:S(2)}, u32[]{:S(2)}) collective-permute-start(bf16[72,4,128]{2,0,1:T(8,128)(2,1)S(1)} %get-tuple-element.27), channel_id=1, source_target_pairs={{0,1},{1,2},{2,3},{4,5},{5,6},{6,7},{8,9},{9,10},{10,11},{12,13},{... | collective-permute-start | bytes 221192 | tf_op jit(solution)/shard_map/ppermute | solution.py:13
  20.3 6.2 %collective-permute-start.6 = (bf16[72,4,128]{2,0,1:T(8,128)(2,1)S(1)}, bf16[72,4,128]{2,0,1:T(8,128)(2,1)S(1)}, u32[]{:S(2)}, u32[]{:S(2)}) collective-permute-start(bf16[72,4,128]{2,0,1:T(8,128)(2,1)S(1)} %get-tuple-element.26), channel_id=1, source_target_pairs={{1,0},{2,1},{3,2},{5,4},{6,5},{7,6},{9,8},{10,9},{11,10},{13,12},{... | collective-permute-start | bytes 221192 | tf_op jit(solution)/shard_map/ppermute | solution.py:16
  26.5 2.1 copy-start.34
  27.0 31.1 %copy-start.6 = (bf16[72,24,136]{2,0,1:T(8,128)(2,1)}, bf16[72,24,136]{2,0,1:T(8,128)(2,1)S(1)}, u32[]{:S(2)}) copy-start(bf16[72,24,136]{2,0,1:T(8,128)(2,1)S(1)} %select_maximum_fusion.10) | copy-start | bytes 1410052
  33.3 3.8 copy-start.22
  33.3 4.4 %copy-start.20 = (bf16[72,7,128]{2,0,1:T(8,128)(2,1)}, bf16[72,7,128]{2,0,1:T(8,128)(2,1)S(1)}, u32[]{:S(2)}) copy-start(bf16[72,7,128]{2,0,1:T(8,128)(2,1)S(1)} %collective-permute-done.1) | copy-start | bytes 387076
  39.2 4.0 %copy-start.3 = (bf16[9,192,192]{2,1,0:T(8,128)(2,1)S(1)}, bf16[9,192,192]{2,1,0:T(8,128)(2,1)}, u32[]{:S(2)}) copy-start(bf16[9,192,192]{2,1,0:T(8,128)(2,1)} %param.12) | copy-start | bytes 1990660
  47.6 3.4 copy-start.14
  54.8 1.7 copy-start.12
  54.8 1.8 copy-start.35
  55.1 4.7 %copy-start.32 = (bf16[72,16,128]{2,1,0:T(8,128)(2,1)S(1)}, bf16[72,16,128]{2,1,0:T(8,128)(2,1)}, u32[]{:S(2)}) copy-start(bf16[72,16,128]{2,1,0:T(8,128)(2,1)} %param.8) | copy-start | bytes 884740
  55.1 4.6 %collective-permute-start.2 = (bf16[72,16,128]{2,0,1:T(8,128)(2,1)S(1)}, bf16[72,16,128]{2,0,1:T(8,128)(2,1)S(1)}, u32[]{:S(2)}, u32[]{:S(2)}) collective-permute-start(bf16[72,16,128]{2,0,1:T(8,128)(2,1)S(1)} %fusion.105), channel_id=1, source_target_pairs={{0,4},{4,8},{8,12},{12,16},{16,20},{20,24},{24,28},{1,5},{5,9},{9,... | collective-permute-start | bytes 884744 | tf_op jit(solution)/shard_map/ppermute | solution.py:24
  59.8 7.4 %collective-permute-start.3 = (bf16[72,7,128]{2,0,1:T(8,128)(2,1)S(1)}, bf16[72,7,128]{2,0,1:T(8,128)(2,1)S(1)}, u32[]{:S(2)}, u32[]{:S(2)}) collective-permute-start(bf16[72,7,128]{2,0,1:T(8,128)(2,1)S(1)} %get-tuple-element.28), channel_id=1, source_target_pairs={{0,1},{1,2},{2,3},{4,5},{5,6},{6,7},{8,9},{9,10},{10,11},{12,13},{... | collective-permute-start | bytes 387080 | tf_op jit(solution)/shard_map/ppermute | solution.py:13
  63.3 6.8 %collective-permute-start.4 = (bf16[72,7,128]{2,0,1:T(8,128)(2,1)S(1)}, bf16[72,7,128]{2,0,1:T(8,128)(2,1)S(1)}, u32[]{:S(2)}, u32[]{:S(2)}) collective-permute-start(bf16[72,7,128]{2,0,1:T(8,128)(2,1)S(1)} %get-tuple-element.29), channel_id=1, source_target_pairs={{1,0},{2,1},{3,2},{5,4},{6,5},{7,6},{9,8},{10,9},{11,10},{13,12},{... | collective-permute-start | bytes 387080 | tf_op jit(solution)/shard_map/ppermute | solution.py:16
  67.2 8.0 %copy-start.26 = (bf16[72,7,128]{2,0,1:T(8,128)(2,1)}, bf16[72,7,128]{2,0,1:T(8,128)(2,1)S(1)}, u32[]{:S(2)}) copy-start(bf16[72,7,128]{2,0,1:T(8,128)(2,1)S(1)} %collective-permute-done.3) | copy-start | bytes 387076
  70.2 5.1 %copy-start.24 = (bf16[72,7,128]{2,0,1:T(8,128)(2,1)}, bf16[72,7,128]{2,0,1:T(8,128)(2,1)S(1)}, u32[]{:S(2)}) copy-start(bf16[72,7,128]{2,0,1:T(8,128)(2,1)S(1)} %collective-permute-done.4) | copy-start | bytes 387076
  85.4 2.1 copy-start.10
  96.2 14.6 %collective-permute-start.8 = (bf16[192,2,128]{2,0,1:T(8,128)(2,1)S(1)}, bf16[192,2,128]{2,0,1:T(8,128)(2,1)S(1)}, u32[]{:S(2)}, u32[]{:S(2)}) collective-permute-start(bf16[192,2,128]{2,0,1:T(8,128)(2,1)S(1)} %get-tuple-element.22), channel_id=1, source_target_pairs={{1,0},{2,1},{3,2},{5,4},{6,5},{7,6},{9,8},{10,9},{11,10},{13,12},{... | collective-permute-start | bytes 294920 | tf_op jit(solution)/shard_map/ppermute | solution.py:16
  97.5 13.3 %collective-permute-start.7 = (bf16[192,2,128]{2,0,1:T(8,128)(2,1)S(1)}, bf16[192,2,128]{2,0,1:T(8,128)(2,1)S(1)}, u32[]{:S(2)}, u32[]{:S(2)}) collective-permute-start(bf16[192,2,128]{2,0,1:T(8,128)(2,1)S(1)} %get-tuple-element.23), channel_id=1, source_target_pairs={{0,1},{1,2},{2,3},{4,5},{5,6},{6,7},{8,9},{9,10},{10,11},{12,13},{... | collective-permute-start | bytes 294920 | tf_op jit(solution)/shard_map/ppermute | solution.py:13
  114.0 1.8 copy-start.8
  117.5 7.0 %copy-start.27 = (bf16[72,7,128]{2,0,1:T(8,128)(2,1)S(1)}, bf16[72,7,128]{2,0,1:T(8,128)(2,1)}, u32[]{:S(2)}) copy-start(bf16[72,7,128]{2,0,1:T(8,128)(2,1)} %copy-done.26) | copy-start | bytes 387076
  117.8 9.1 %collective-permute-start.10 = (bf16[192,1,128]{2,0,1:T(8,128)(2,1)S(1)}, bf16[192,1,128]{2,0,1:T(8,128)(2,1)S(1)}, u32[]{:S(2)}, u32[]{:S(2)}) collective-permute-start(bf16[192,1,128]{2,0,1:T(8,128)(2,1)S(1)} %get-tuple-element.21), channel_id=1, source_target_pairs={{1,0},{2,1},{3,2},{5,4},{6,5},{7,6},{9,8},{10,9},{11,10},{13,12},{... | collective-permute-start | bytes 147464 | tf_op jit(solution)/shard_map/ppermute | solution.py:16
  119.1 7.8 %collective-permute-start.9 = (bf16[192,1,128]{2,0,1:T(8,128)(2,1)S(1)}, bf16[192,1,128]{2,0,1:T(8,128)(2,1)S(1)}, u32[]{:S(2)}, u32[]{:S(2)}) collective-permute-start(bf16[192,1,128]{2,0,1:T(8,128)(2,1)S(1)} %get-tuple-element.20), channel_id=1, source_target_pairs={{0,1},{1,2},{2,3},{4,5},{5,6},{6,7},{8,9},{9,10},{10,11},{12,13},{... | collective-permute-start | bytes 147464 | tf_op jit(solution)/shard_map/ppermute | solution.py:13
  130.3 1.8 copy-start.25
  130.7 3.6 copy-start.33
  130.7 3.6 collective-permute-start.11
  138.2 7.4 %collective-permute-start.13 = (bf16[72,4,128]{2,0,1:T(8,128)(2,1)S(1)}, bf16[72,4,128]{2,0,1:T(8,128)(2,1)S(1)}, u32[]{:S(2)}, u32[]{:S(2)}) collective-permute-start(bf16[72,4,128]{2,0,1:T(8,128)(2,1)S(1)} %get-tuple-element.24), channel_id=1, source_target_pairs={{1,0},{2,1},{3,2},{5,4},{6,5},{7,6},{9,8},{10,9},{11,10},{13,12},{... | collective-permute-start | bytes 221192 | tf_op jit(solution)/shard_map/ppermute | solution.py:16
  139.5 6.5 %collective-permute-start.12 = (bf16[72,4,128]{2,0,1:T(8,128)(2,1)S(1)}, bf16[72,4,128]{2,0,1:T(8,128)(2,1)S(1)}, u32[]{:S(2)}, u32[]{:S(2)}) collective-permute-start(bf16[72,4,128]{2,0,1:T(8,128)(2,1)S(1)} %get-tuple-element.25), channel_id=1, source_target_pairs={{0,1},{1,2},{2,3},{4,5},{5,6},{6,7},{8,9},{9,10},{10,11},{12,13},{... | collective-permute-start | bytes 221192 | tf_op jit(solution)/shard_map/ppermute | solution.py:13
  156.6 8.4 %collective-permute-start.15 = (bf16[192,2,128]{2,0,1:T(8,128)(2,1)S(1)}, bf16[192,2,128]{2,0,1:T(8,128)(2,1)S(1)}, u32[]{:S(2)}, u32[]{:S(2)}) collective-permute-start(bf16[192,2,128]{2,0,1:T(8,128)(2,1)S(1)} %get-tuple-element.18), channel_id=1, source_target_pairs={{1,0},{2,1},{3,2},{5,4},{6,5},{7,6},{9,8},{10,9},{11,10},{13,12},{... | collective-permute-start | bytes 294920 | tf_op jit(solution)/shard_map/ppermute | solution.py:16
  157.9 7.1 %collective-permute-start.14 = (bf16[192,2,128]{2,0,1:T(8,128)(2,1)S(1)}, bf16[192,2,128]{2,0,1:T(8,128)(2,1)S(1)}, u32[]{:S(2)}, u32[]{:S(2)}) collective-permute-start(bf16[192,2,128]{2,0,1:T(8,128)(2,1)S(1)} %get-tuple-element.19), channel_id=1, source_target_pairs={{0,1},{1,2},{2,3},{4,5},{5,6},{6,7},{8,9},{9,10},{10,11},{12,13},{... | collective-permute-start | bytes 294920 | tf_op jit(solution)/shard_map/ppermute | solution.py:13
  167.8 1.8 copy-start.7
  169.5 2.1 copy-start.5
  169.6 2.1 copy-start.23
  175.8 201.5 %all-reduce.21.cloned.1.call-start = ((), (), s32[]{:S(2)}) async-start(), calls=%async_computation | async-start | bytes 6193152 | tf_op jit(solution)/shard_map/psum | solution.py:131
  175.9 2.5 copy-start.19
  181.2 6.8 %collective-permute-start.17 = (bf16[192,1,128]{2,0,1:T(8,128)(2,1)S(1)}, bf16[192,1,128]{2,0,1:T(8,128)(2,1)S(1)}, u32[]{:S(2)}, u32[]{:S(2)}) collective-permute-start(bf16[192,1,128]{2,0,1:T(8,128)(2,1)S(1)} %get-tuple-element.17), channel_id=1, source_target_pairs={{1,0},{2,1},{3,2},{5,4},{6,5},{7,6},{9,8},{10,9},{11,10},{13,12},{... | collective-permute-start | bytes 147464 | tf_op jit(solution)/shard_map/ppermute | solution.py:16
  182.8 6.7 %collective-permute-start.16 = (bf16[192,1,128]{2,0,1:T(8,128)(2,1)S(1)}, bf16[192,1,128]{2,0,1:T(8,128)(2,1)S(1)}, u32[]{:S(2)}, u32[]{:S(2)}) collective-permute-start(bf16[192,1,128]{2,0,1:T(8,128)(2,1)S(1)} %get-tuple-element.16), channel_id=1, source_target_pairs={{0,1},{1,2},{2,3},{4,5},{5,6},{6,7},{8,9},{9,10},{10,11},{12,13},{... | collective-permute-start | bytes 147464 | tf_op jit(solution)/shard_map/ppermute | solution.py:13
  305.3 1.8 copy-start.2
  305.6 2.0 copy-start.31
  377.3 2.9 copy-start.29
  377.3 2.9 copy-start.30
  (8 other events, 10.9 us)
Sparse Core Ops, SparseCore 0:
  176.0 129.2 all-reduce.22
  308.9 68.3 all-reduce.20
